TPU v7x, 512 devices: a whole 4x8x8 slice. The times are simulated.
512 devices in a mesh: ctx: 32 (over z_lo, x, core), tp: 16 (over z_hi, y).
Axes of the slice: x: 4, y: 8, z: 8 (z_hi: 2, z_lo: 4; z = z_hi * 4 + z_lo), core: 2. Of those that a mesh axis runs over, the one named last changes fastest.
Arguments:
- queries: bfloat16 [8192, 8192], P('ctx', 'tp'), may hold values from -100 to 100
- key_rows: bfloat16 [8192, 1024], P('ctx'), may hold values from -5 to 5
- value_rows: bfloat16 [8192, 1024], P('ctx'), may hold values from -6 to 6
- documents: int32 [8192], P('ctx'), may hold values from 0 to 3, never falling along the last dimension, each value on 1 to 6144 neighbouring positions
- out_weight: bfloat16 [8192, 8192], P('tp', 'ctx'), may hold values from -0.75 to 0.75
Outputs:
- attention_out: bfloat16 [8192, 8192], P(('ctx', 'tp'))
Inputs may be any that keep to these rules, and one draw needn't show every extreme that they name: `documents`: document numbers never fall along the window; each document holds 1 to 6144 tokens and one holds exactly 6144.
All inputs are finite; a program needn't handle non-finite values.
Results may differ from a plain program's by a relative error of at most 0.015.
Values may be sent and summed in bfloat16 or wider, within the bound.
No kernel may reach another device: no remote copies, remote signals or barrier semaphores. Data moves between devices by JAX's collectives and lax.ppermute only.
A program may use at most 128 MiB of HBM per device.

v0:
```python
import math
import jax
import jax.numpy as jnp
from jax import lax
from jax.sharding import PartitionSpec as P

HEADS = 64
KV_HEADS = 8
HD = 128


def absorb_group(state, query_block, query_pos, query_docs, piece, start):
    piece_keys, piece_values, piece_docs = piece
    length = piece_keys.shape[0]
    kv_here = query_block.shape[1]
    scale = 1.0 / math.sqrt(HD)

    def update(inner):
        old_max, old_sum, old_acc = inner
        key_block = piece_keys.reshape(length, kv_here, HD)
        value_block = piece_values.reshape(length, kv_here, HD)
        scores = (
            jnp.einsum("tghd,ngd->ghtn", query_block, key_block, preferred_element_type=jnp.float32)
            * scale
        )
        key_pos = jnp.arange(length, dtype=jnp.int32)
        allowed = (key_pos[None, :] <= query_pos[:, None]) & (
            piece_docs[None, :] == query_docs[:, None]
        )
        new_max = jnp.maximum(old_max, jnp.max(jnp.where(allowed, scores, -1e30), axis=3))
        weights = jnp.where(allowed, jnp.exp(scores - new_max[..., None]), 0.0)
        new_sum = jnp.sum(weights, axis=3)
        weighted = jnp.einsum(
            "ghtn,ngd->tghd",
            weights.astype(jnp.bfloat16),
            value_block,
            preferred_element_type=jnp.float32,
        )
        return (new_max, new_sum, weighted)

    return lax.cond(start <= query_pos[-1], update, lambda inner: inner, state)


def empty_state(rows, kv_here, per_kv):
    return (
        jnp.full((kv_here, per_kv, rows), -1e30, jnp.float32),
        jnp.zeros((kv_here, per_kv, rows), jnp.float32),
        jnp.zeros((rows, kv_here, per_kv, HD), jnp.float32),
    )


def finish(state):
    run_max, run_sum, run_acc = state
    rows = run_acc.shape[0]
    attended = (run_acc / jnp.transpose(run_sum, (2, 0, 1))[..., None]).astype(jnp.bfloat16)
    return attended.reshape(rows, run_acc.shape[1] * run_acc.shape[2] * HD)


def on_device(queries, key_rows, value_rows, documents, out_weight):
    tokens_here = queries.shape[0]
    heads_here = queries.shape[1] // HD
    group_size = HEADS // KV_HEADS
    kv_here = max(1, heads_here // group_size)
    per_kv = heads_here // kv_here
    kv_first = lax.axis_index("tp") * heads_here // group_size
    own_keys = lax.dynamic_slice_in_dim(key_rows, kv_first * HD, kv_here * HD, 1)
    own_values = lax.dynamic_slice_in_dim(value_rows, kv_first * HD, kv_here * HD, 1)
    query_blocks = queries.reshape(tokens_here, kv_here, per_kv, HD)
    first_row = lax.axis_index("ctx") * tokens_here
    groups = [(query_blocks, first_row + jnp.arange(tokens_here, dtype=jnp.int32), documents)]
    initial = tuple((empty_state(group[0].shape[0], kv_here, per_kv) for group in groups))
    piece = (
        lax.all_gather(own_keys, "ctx", axis=0, tiled=True),
        lax.all_gather(own_values, "ctx", axis=0, tiled=True),
        lax.all_gather(documents, "ctx", axis=0, tiled=True),
    )
    start = jnp.int32(0)
    states = tuple(
        (
            absorb_group(
                initial[index], groups[index][0], groups[index][1], groups[index][2], piece, start
            )
            for index in range(len(groups))
        )
    )
    attended = finish(states[0])
    terms = jnp.dot(
        attended,
        lax.all_gather(out_weight, "ctx", axis=1, tiled=True),
        preferred_element_type=jnp.float32,
    )
    summed = lax.psum_scatter(terms.astype(jnp.bfloat16), "tp", scatter_dimension=0, tiled=True)
    return summed


def solution(mesh):
    in_specs = (P("ctx", "tp"), P("ctx", None), P("ctx", None), P("ctx"), P("tp", "ctx"))
    out_specs = P(("ctx", "tp"), None)
    return jax.shard_map(
        on_device, mesh=mesh, in_specs=in_specs, out_specs=out_specs, check_vma=False
    )
```

profile of v0, /device:TPU:2, one launch (start us, length us, event | category | flops | bytes accessed | tf_op | source)
XLA Modules:
  0.0 487.1 jit_solution(4593538375489686162)
XLA Ops:
  6.5 0.0 copy-start
  6.5 0.0 all-gather.5.cloned.1.call-start
  6.5 1.0 copy-done
  7.6 0.6 constant_dynamic-slice_fusion.1
  8.2 0.0 all-gather.5.cloned.1.call-update
  8.2 0.0 all-gather.7.cloned.1.call-start
  8.3 1.5 constant_dynamic-slice_fusion
  9.8 0.0 all-gather.7.cloned.1.call-update
  9.8 0.0 all-gather.9.cloned.1.call-start
  9.8 0.7 all-gather.9.cloned.1.call-update
  10.5 0.0 reduce-scatter.2.cloned.1.call-start
  10.6 0.6 slice.3
  11.9 43.7 %all-gather = s32[32,1,256]{2,1,0:T(1,128)S(1)} all-gather(s32[1,1,256]{2,1,0:T(1,128)} %bitcast.64), channel_id=1, replica_groups=mesh['ctx'=32,'tp'=16] {'ctx'}, dimensions={0}, use_global_device_ids=true | all-gather | bytes 33792 | tf_op jit(solution)/shard_map/all_gather | solution.py:75
  55.6 21.2 %all-gather.5.cloned.1.call-done = bf16[8192,128]{1,0:T(8,128)(2,1)} async-done(((bf16[256,128]{1,0:T(8,128)(2,1)}), bf16[8192,128]{1,0:T(8,128)(2,1)}) %all-gather.5.cloned.1.call-update) | async-done | bytes 2097168 | tf_op jit(solution)/shard_map/all_gather | solution.py:73
  76.7 63.6 %all-gather.7.cloned.1.call-done = bf16[8192,128]{1,0:T(8,128)(2,1)} async-done(((bf16[256,128]{1,0:T(8,128)(2,1)}), bf16[8192,128]{1,0:T(8,128)(2,1)}) %all-gather.7.cloned.1.call-update) | async-done | bytes 2097168 | tf_op jit(solution)/shard_map/all_gather | solution.py:74
  140.4 49.9 %conditional.1 = (f32[1,4,256]{2,1,0:T(4,128)S(1)}, f32[256,1,4,128]{0,3,2,1:T(8,128)S(1)}) conditional(s32[]{:T(128)} %bitcast.10, () %tuple.13, (s32[256]{0:T(256)S(1)}, s32[8192]{0:T(1024)S(1)}, s32[256]{0:T(256)}, bf16[256,512]{1,0:T(8,128)(2,1)}, bf16[8192,128]{1,0:T(8,128)(2,1)}, /*index=5*/bf16[8192,128]{1,0:T(8,128)(2,1)}) %tuple.28), branch_computations={%region_0.1_spmd, %region_1.4_spmd} | conditional | flops 4393532416 | bytes 115140624 | solution.py:41
  140.4 4.4 fusion.9
  144.8 14.9 %fusion = (f32[4,256]{1,0:T(4,128)S(1)}, f32[8192,256,4]{1,0,2:T(8,128)}) fusion(pred[256,8192]{0,1:T(8,128)(4,1)S(1)} %fusion.9, bf16[8192,128]{1,0:T(8,128)(2,1)} %get-tuple-element.21, bf16[256,512]{1,0:T(8,128)(2,1)} %get-tuple-element.29), kind=kOutput, calls=%fused_computation.2 | convolution fusion | flops 2172648448 | bytes 38014976 | tf_op jit(solution)/shard_map/cond/branch_1_fun/tghd,ngd->ghtn/dot_general | solution.py:23
  159.8 14.8 %fusion.4 = f32[4,256]{1,0:T(4,128)S(1)} fusion(f32[8192,256,4]{1,0,2:T(8,128)} %get-tuple-element.32, f32[4,256]{1,0:T(4,128)S(1)} %broadcast_maximum_fusion, pred[256,8192]{0,1:T(8,128)(4,1)S(1)} %fusion.9), kind=kLoop, calls=%fused_computation.6 | loop fusion | flops 33553408 | bytes 35659776 | tf_op jit(solution)/shard_map/cond/branch_1_fun/reduce_sum | solution.py:32
  174.5 15.5 %fusion.13 = f32[256,1,4,128]{3,0,2,1:T(8,128)S(1)} fusion(bf16[8192,128]{1,0:T(8,128)(2,1)} %get-tuple-element.23, f32[8192,256,4]{1,0,2:T(8,128)} %get-tuple-element.32, f32[4,256]{1,0:T(4,128)S(1)} %broadcast_maximum_fusion, pred[256,8192]{0,1:T(8,128)(4,1)S(1)} %fusion.9), kind=kOutput, calls=%fused_computation.15 | convolution fusion | flops 2181038080 | bytes 38277120 | tf_op jit(solution)/shard_map/cond/branch_1_fun/ghtn,ngd->tghd/dot_general | solution.py:33
  190.1 0.2 copy.17
  190.3 40.4 %all-gather.9.cloned.1.call-done = bf16[512,8192]{1,0:T(8,128)(2,1)} async-done(((bf16[512,256]{1,0:T(8,128)(2,1)}), bf16[512,8192]{1,0:T(8,128)(2,1)}) %all-gather.9.cloned.1.call-update) | async-done | bytes 8388624 | tf_op jit(solution)/shard_map/all_gather | solution.py:89
  230.7 7.7 %convolution_convert_fusion = bf16[256,8192]{1,0:T(8,128)(2,1)} fusion(bf16[256,512]{0,1:T(8,128)(2,1)S(1)} %bitcast.60, bf16[512,8192]{1,0:T(8,128)(2,1)} %all-gather.9.cloned.1.call-done), kind=kOutput, calls=%fused_computation.21 | convolution fusion | flops 2149580800 | bytes 12845056 | tf_op jit(solution)/shard_map/dot_general | solution.py:87
  238.4 0.0 reduce-scatter.2.cloned.1.call-update
  238.5 242.1 %reduce-scatter.2.cloned.1.call-done = bf16[16,8192]{1,0:T(8,128)(2,1)} async-done(((bf16[256,8192]{1,0:T(8,128)(2,1)}), bf16[16,8192]{1,0:T(8,128)(2,1)}) %reduce-scatter.2.cloned.1.call-update) | async-done | bytes 262160 | tf_op jit(solution)/shard_map/reduce_scatter | solution.py:92
  (3 shorter events, 0.1 us)
Async XLA Ops:
  6.5 1.0 copy-start
  6.5 70.2 %all-gather.5.cloned.1.call-start = ((), (), s32[]{:S(2)}) async-start(), calls=%async_computation.1 | async-start | bytes 2162688 | tf_op jit(solution)/shard_map/all_gather | solution.py:73
  8.2 132.1 %all-gather.7.cloned.1.call-start = ((), (), s32[]{:S(2)}) async-start(), calls=%async_computation.2 | async-start | bytes 2162688 | tf_op jit(solution)/shard_map/all_gather | solution.py:74
  9.8 220.9 %all-gather.9.cloned.1.call-start = ((), (), s32[]{:S(2)}) async-start(), calls=%async_computation.3 | async-start | bytes 8650752 | tf_op jit(solution)/shard_map/all_gather | solution.py:89
  10.5 470.1 %reduce-scatter.2.cloned.1.call-start = ((), (), s32[]{:S(2)}) async-start(), calls=%async_computation.4 | async-start | bytes 4456448 | tf_op jit(solution)/shard_map/reduce_scatter | solution.py:92
Sparse Core Ops, SparseCore 0:
  9.5 67.2 all-gather.4
  78.9 61.4 all-gather.6
  142.4 88.2 all-gather.8
  238.6 241.9 reduce-scatter.1
where the time goes:
time: 488 us; the launch traced here: 487 us
  waiting for transfers between devices  368 us (75%)
  blocking collectives  43.7 us (9%)
  matrix products  38.2 us (8%)
  other arithmetic  19.2 us (4%)
  between operations  13.8 us (3%)
    reduce_scatter x1, waiting for transfers between devices, on_device(): lax.psum_scatter(terms.astype(jnp.bfloat16), 'tp', scatter_dimension=0, t...  242 us
    all_gather x1, waiting for transfers between devices, on_device(): lax.all_gather(own_values, 'ctx', axis=0, tiled=True)  63.6 us
    all_gather x1, blocking collectives, on_device(): lax.all_gather(documents, 'ctx', axis=0, tiled=True)  43.7 us
    all_gather x1, waiting for transfers between devices, on_device(): lax.all_gather(out_weight, 'ctx', axis=1, tiled=True)  40.4 us
    all_gather x1, waiting for transfers between devices, on_device(): lax.all_gather(own_keys, 'ctx', axis=0, tiled=True)  21.2 us
    dot_general x1, matrix products, update(): jnp.einsum('ghtn,ngd->tghd', weights.astype(jnp.bfloat16), value_block, p...  15.5 us
    dot_general x1, matrix products, update(): jnp.einsum('tghd,ngd->ghtn', query_block, key_block, preferred_element_ty...  14.9 us
    reduce_sum x1, other arithmetic, update(): new_sum = jnp.sum(weights, axis=3)  14.8 us
  transfers between devices with their start and end apart: 4, of which 4 were waited for; matrix products, arithmetic and copies ran while one was open for 11% of the time, Pallas kernels for 0%

commit v1 on v0

--- a/solution.py
+++ b/solution.py
@@ -69,9 +69,18 @@
     first_row = lax.axis_index("ctx") * tokens_here
     groups = [(query_blocks, first_row + jnp.arange(tokens_here, dtype=jnp.int32), documents)]
     initial = tuple((empty_state(group[0].shape[0], kv_here, per_kv) for group in groups))
+    tell_frames = lambda my_tile: jnp.concatenate(
+        lax.all_to_all(
+            jnp.stack([my_tile for _ in range(lax.axis_size("ctx"))]),
+            concat_axis=0,
+            split_axis=0,
+            axis_name="ctx",
+        ),
+        axis=0,
+    )
     piece = (
         lax.all_gather(own_keys, "ctx", axis=0, tiled=True),
-        lax.all_gather(own_values, "ctx", axis=0, tiled=True),
+        tell_frames(own_values),
         lax.all_gather(documents, "ctx", axis=0, tiled=True),
     )
     start = jnp.int32(0)

time: 488 us -> 438 us (0.90)
  waiting for transfers between devices: 368 us -> 273 us
  blocking collectives: 43.7 us -> 75.5 us
  starting transfers between devices: 0.12 us -> 10.5 us
    all_gather x1 -> x0, waiting for transfers between devices: 63.6 us -> none  [on_device(): lax.all_gather(own_values, 'ctx', axis=0, tiled=True)]
    all_gather x1, blocking collectives: 43.7 us -> 75.5 us  [on_device(): lax.all_gather(documents, 'ctx', axis=0, tiled=True)]
    all_gather x1, waiting for transfers between devices: 21.2 us -> 0.01 us  [on_device(): lax.all_gather(own_keys, 'ctx', axis=0, tiled=True)]
    all_gather x1, waiting for transfers between devices: 40.4 us -> 29.7 us  [on_device(): lax.all_gather(out_weight, 'ctx', axis=1, tiled=True)]
    all_to_all x0 -> x1, starting transfers between devices: none -> 10.4 us  [on_device(): lax.all_to_all(jnp.stack([my_tile for _ in range(lax.axis_size('ctx'))]),...]
  transfers between devices with their start and end apart: 4 -> 4, of which waited for: 4 -> 2; matrix products, arithmetic and copies ran while one was open for 11% -> 12% of each run, Pallas kernels for 0% -> 0%
where the time goes in v1:
time: 438 us
  waiting for transfers between devices  273 us (62%)
  blocking collectives  75.5 us (17%)
  matrix products  38.2 us (9%)
  other arithmetic  19.4 us (4%)
  between operations  13.8 us (3%)
  starting transfers between devices  10.5 us (2%)
  local copies, waits for them, and re-layouts  7.54 us (2%)
    reduce_scatter x1, waiting for transfers between devices, on_device(): lax.psum_scatter(terms.astype(jnp.bfloat16), 'tp', scatter_dimension=0, t...  242 us
    all_gather x1, blocking collectives, on_device(): lax.all_gather(documents, 'ctx', axis=0, tiled=True)  75.5 us
    all_gather x1, waiting for transfers between devices, on_device(): lax.all_gather(out_weight, 'ctx', axis=1, tiled=True)  29.7 us
    dot_general x1, matrix products, update(): jnp.einsum('ghtn,ngd->tghd', weights.astype(jnp.bfloat16), value_block, p...  15.4 us
    dot_general x1, matrix products, update(): jnp.einsum('tghd,ngd->ghtn', query_block, key_block, preferred_element_ty...  15 us
    reduce_sum x1, other arithmetic, update(): new_sum = jnp.sum(weights, axis=3)  14.9 us
    all_to_all x1, starting transfers between devices, on_device(): lax.all_to_all(jnp.stack([my_tile for _ in range(lax.axis_size('ctx'))]),...  10.4 us
  transfers between devices with their start and end apart: 4, of which 2 were waited for; matrix products, arithmetic and copies ran while one was open for 12% of the time, Pallas kernels for 0%

profile of v1, /device:TPU:2, one launch (start us, length us, event | category | flops | bytes accessed | tf_op | source)
XLA Modules:
  0.0 437.6 jit_solution(7548260403864477587)
XLA Ops:
  6.5 0.0 copy-start
  6.5 0.0 all-gather.4.cloned.1.call-start
  6.5 1.0 copy-done
  7.6 0.6 constant_dynamic-slice_fusion.1
  8.2 0.0 all-gather.4.cloned.1.call-update
  8.2 0.0 all-gather.6.cloned.1.call-start
  8.3 0.7 all-gather.6.cloned.1.call-update
  9.0 0.9 constant_dynamic-slice_fusion
  9.9 1.8 stack.2
  11.7 10.4 %all-to-all-start = ((bf16[32,256,128]{2,1,0:T(8,128)(2,1)}), bf16[32,256,128]{2,1,0:T(8,128)(2,1)S(1)}, u32[]{:S(2)}, u32[]{:S(2)}) async-start(bf16[32,256,128]{2,1,0:T(8,128)(2,1)} %stack.2), calls=%async_computation | async-start | bytes 4194304 | tf_op jit(solution)/shard_map/all_to_all | solution.py:73
  22.1 0.0 reduce-scatter.2.cloned.1.call-start
  22.2 0.6 slice.3
  23.5 75.5 %all-gather = s32[32,1,256]{2,1,0:T(1,128)S(1)} all-gather(s32[1,1,256]{2,1,0:T(1,128)} %bitcast.64), channel_id=1, replica_groups=mesh['ctx'=32,'tp'=16] {'ctx'}, dimensions={0}, use_global_device_ids=true | all-gather | bytes 33792 | tf_op jit(solution)/shard_map/all_gather | solution.py:84
  99.0 0.0 all-gather.4.cloned.1.call-done
  99.0 0.0 all-to-all-done
  99.0 52.4 %conditional.1 = (f32[1,4,256]{2,1,0:T(4,128)S(1)}, f32[256,1,4,128]{0,3,2,1:T(8,128)S(1)}) conditional(s32[]{:T(128)} %bitcast.11, () %tuple.13, (s32[256]{0:T(256)S(1)}, s32[8192]{0:T(1024)S(1)}, s32[256]{0:T(256)}, bf16[256,512]{1,0:T(8,128)(2,1)}, bf16[8192,128]{1,0:T(8,128)(2,1)}, /*index=5*/bf16[32,256,128]{2,1,0:T(8,128)(2,1)S(1)}) %tuple.26), branch_computations={%region_0.1_spmd, %region_1.4_spmd} | conditional | flops 4393532416 | bytes 131917896 | solution.py:41
  99.0 0.0 copy-start.1
  99.0 1.3 copy-done.1
  100.3 4.4 %fusion.9 = pred[256,8192]{0,1:T(8,128)(4,1)S(1)} fusion(s32[256]{0:T(256)} %get-tuple-element.20, s32[256]{0:T(256)S(1)} %get-tuple-element.18, s32[8192]{0:T(1024)S(1)} %get-tuple-element.19), kind=kLoop, calls=%fused_computation.11 | loop fusion | flops 6291456 | bytes 2131968 | tf_op jit(solution)/shard_map/cond/branch_1_fun/and | solution.py:27
  104.7 15.0 %fusion = (f32[4,256]{1,0:T(4,128)S(1)}, f32[8192,256,4]{1,0,2:T(8,128)}) fusion(pred[256,8192]{0,1:T(8,128)(4,1)S(1)} %fusion.9, bf16[8192,128]{1,0:T(8,128)(2,1)} %get-tuple-element.21, bf16[256,512]{1,0:T(8,128)(2,1)} %get-tuple-element.29), kind=kOutput, calls=%fused_computation.2 | convolution fusion | flops 2172648448 | bytes 38014976 | tf_op jit(solution)/shard_map/cond/branch_1_fun/tghd,ngd->ghtn/dot_general | solution.py:23
  119.8 0.0 copy-start.2
  119.8 14.9 %fusion.4 = f32[4,256]{1,0:T(4,128)S(1)} fusion(f32[8192,256,4]{1,0,2:T(8,128)} %get-tuple-element.32, f32[4,256]{1,0:T(4,128)S(1)} %broadcast_maximum_fusion, pred[256,8192]{0,1:T(8,128)(4,1)S(1)} %fusion.9), kind=kLoop, calls=%fused_computation.6 | loop fusion | flops 33553408 | bytes 35659776 | tf_op jit(solution)/shard_map/cond/branch_1_fun/reduce_sum | solution.py:32
  134.7 0.0 copy-done.2
  134.7 15.4 %fusion.12 = f32[256,1,4,128]{3,0,2,1:T(8,128)} fusion(bf16[8192,128,1]{1,0,2:T(8,128)(2,1)S(1)} %bitcast.59, f32[8192,256,4]{1,0,2:T(8,128)} %get-tuple-element.32, f32[4,256]{1,0:T(4,128)S(1)} %broadcast_maximum_fusion, pred[256,8192]{0,1:T(8,128)(4,1)S(1)} %fusion.9), kind=kOutput, calls=%fused_computation.14 | convolution fusion | flops 2181038080 | bytes 38277120 | tf_op jit(solution)/shard_map/cond/branch_1_fun/ghtn,ngd->tghd/dot_general | solution.py:33
  150.1 1.2 copy.17
  151.4 29.7 %all-gather.6.cloned.1.call-done = bf16[512,8192]{1,0:T(8,128)(2,1)} async-done(((bf16[512,256]{1,0:T(8,128)(2,1)}), bf16[512,8192]{1,0:T(8,128)(2,1)}) %all-gather.6.cloned.1.call-update) | async-done | bytes 8388624 | tf_op jit(solution)/shard_map/all_gather | solution.py:98
  181.1 7.7 %convolution_convert_fusion = bf16[256,8192]{1,0:T(8,128)(2,1)} fusion(bf16[256,512]{0,1:T(8,128)(2,1)S(1)} %bitcast.60, bf16[512,8192]{1,0:T(8,128)(2,1)} %all-gather.6.cloned.1.call-done), kind=kOutput, calls=%fused_computation.20 | convolution fusion | flops 2149580800 | bytes 12845056 | tf_op jit(solution)/shard_map/dot_general | solution.py:96
  188.8 0.0 reduce-scatter.2.cloned.1.call-update
  188.8 242.2 %reduce-scatter.2.cloned.1.call-done = bf16[16,8192]{1,0:T(8,128)(2,1)} async-done(((bf16[256,8192]{1,0:T(8,128)(2,1)}), bf16[16,8192]{1,0:T(8,128)(2,1)}) %reduce-scatter.2.cloned.1.call-update) | async-done | bytes 262160 | tf_op jit(solution)/shard_map/reduce_scatter | solution.py:101
  (3 shorter events, 0.1 us)
Async XLA Ops:
  6.5 1.0 copy-start
  6.5 92.5 %all-gather.4.cloned.1.call-start = ((), (), s32[]{:S(2)}) async-start(), calls=%async_computation.2 | async-start | bytes 2162688 | tf_op jit(solution)/shard_map/all_gather | solution.py:82
  8.2 172.9 %all-gather.6.cloned.1.call-start = ((), (), s32[]{:S(2)}) async-start(), calls=%async_computation.3 | async-start | bytes 8650752 | tf_op jit(solution)/shard_map/all_gather | solution.py:98
  11.7 87.3 %all-to-all-start = ((bf16[32,256,128]{2,1,0:T(8,128)(2,1)}), bf16[32,256,128]{2,1,0:T(8,128)(2,1)S(1)}, u32[]{:S(2)}, u32[]{:S(2)}) async-start(bf16[32,256,128]{2,1,0:T(8,128)(2,1)} %stack.2), calls=%async_computation | async-start | bytes 4194304 | tf_op jit(solution)/shard_map/all_to_all | solution.py:73
  22.1 408.9 %reduce-scatter.2.cloned.1.call-start = ((), (), s32[]{:S(2)}) async-start(), calls=%async_computation.4 | async-start | bytes 4456448 | tf_op jit(solution)/shard_map/reduce_scatter | solution.py:101
  99.0 1.3 copy-start.1
  119.8 14.9 %copy-start.2 = (bf16[32,256,128]{2,1,0:T(8,128)(2,1)S(1)}, bf16[32,256,128]{2,1,0:T(8,128)(2,1)}, u32[]{:S(2)}) copy-start(bf16[32,256,128]{2,1,0:T(8,128)(2,1)} %copy-done.1) | copy-start | bytes 6291460 | tf_op jit(solution)/shard_map/cond
Sparse Core Ops, SparseCore 0:
  9.5 78.1 all-gather.3
  89.8 91.2 all-gather.5
  188.9 242.0 reduce-scatter.1
